TPU v7x, 32 devices: a whole 2x2x4 slice. The times are simulated.
32 devices in a mesh: sec: 4 (over y, x), dev: 8 (over z, core).
Axes of the slice: x: 2, y: 2, z: 4, core: 2. Of those that a mesh axis runs over, the one named last changes fastest.
Arguments:
- child_panel: bfloat16 [4, 6144, 2048], P('sec', 'dev'), may hold values from -0.23925781 to 0.23925781
- child_inverse: bfloat16 [4, 2048, 2048], P('sec'), may hold values from -0.03756505 to 1.5, as said below
- child_map: int32 [4, 48], replicated, may hold values from 0 to 63, as said below
- parent_front: bfloat16 [8192, 8192], P('sec', 'dev'), may hold values from -6 to 6
- parent_inverse: bfloat16 [1024, 1024], replicated, may hold values from -0.00166015625 to 0.046875, as said below
- parent_pivots: int32 [8], replicated, may hold values from 0 to 63, as said below
Outputs:
- parent_update: float32 [8192, 8192], P('sec', 'dev')
- parent_factor: bfloat16 [8192, 1024], P('sec')
Inputs may be any that keep to these rules, and one draw needn't show every extreme that they name: `child_map`: each row names 48 different parent blocks. `parent_pivots`: 8 different parent blocks. `child_inverse`: upper triangular with positive diagonal. `parent_inverse`: upper triangular with positive diagonal.
All inputs are finite; a program needn't handle non-finite values.
Results may differ from a plain program's by a relative error of at most 0.014.
Values may be sent and summed in bfloat16 or wider, within the bound.
A program may use at most 128 MiB of HBM per device.

v0:
```python
import jax
import jax.numpy as jnp
from jax import lax
from jax.sharding import PartitionSpec as P

BLK = 128
PORD = 8192


def spread_2(value, axis, source):
    kept = jnp.where(lax.axis_index(axis) == source, value, 0).astype(value.dtype)
    return lax.psum(kept, axis)


def outer_rows(left_rows, right_rows):
    return lax.dot_general(
        left_rows, right_rows, (((1,), (1,)), ((), ())), preferred_element_type=jnp.float32
    )


def local(child_panel, child_inverse, child_map, parent_front, parent_inverse, parent_pivots):
    dev_count = lax.axis_size("dev")
    sec_count = lax.axis_size("sec")
    sec_index = lax.axis_index("sec")
    dev_index = lax.axis_index("dev")
    block_count = PORD // BLK
    cols_dev = block_count // dev_count
    rows_sec = block_count // sec_count
    col_width = cols_dev * BLK
    my_map = lax.dynamic_index_in_dim(child_map, sec_index, 0, keepdims=False)
    child_blocks = my_map.shape[0]
    place_map = (my_map[:, None] == jnp.arange(block_count, dtype=jnp.int32)[None, :]).astype(
        jnp.bfloat16
    )
    lower_rows = jnp.dot(
        child_panel[0], child_inverse[0], preferred_element_type=jnp.float32
    ).astype(jnp.bfloat16)
    col_targets = dev_index * cols_dev + jnp.arange(cols_dev, dtype=jnp.int32)
    whole_rows = lax.all_gather(lower_rows, "dev", axis=0, tiled=True)
    pick_cols = (my_map[None, :] == col_targets[:, None]).astype(jnp.bfloat16)
    chosen = jnp.einsum(
        "mj,jbp->mbp",
        pick_cols,
        whole_rows.reshape(child_blocks, BLK, -1),
        preferred_element_type=jnp.float32,
    ).astype(jnp.bfloat16)
    by_columns = (-outer_rows(whole_rows, chosen.reshape(col_width, -1))).astype(jnp.bfloat16)
    spread = jnp.einsum(
        "jm,jbc->mbc",
        place_map,
        by_columns.reshape(child_blocks, BLK, col_width),
        preferred_element_type=jnp.float32,
    ).reshape(PORD, col_width)
    summed = lax.psum_scatter(
        spread.astype(jnp.bfloat16), "sec", scatter_dimension=0, tiled=True
    ).astype(jnp.float32)
    assembled = parent_front.astype(jnp.float32) + summed
    panel_values = assembled.astype(jnp.bfloat16)
    pivot_blocks = parent_pivots.shape[0]
    pick_pivots = (parent_pivots[None, :] == col_targets[:, None]).astype(jnp.bfloat16)
    selected = jnp.einsum(
        "mr,rbk->mbk",
        pick_pivots,
        parent_inverse.reshape(pivot_blocks, BLK, -1),
        preferred_element_type=jnp.float32,
    ).astype(jnp.bfloat16)
    partial_sum = jnp.dot(
        panel_values, selected.reshape(col_width, -1), preferred_element_type=jnp.float32
    )
    parent_factor = lax.psum(partial_sum.astype(jnp.bfloat16), "dev")
    my_blocks = sec_index * rows_sec + jnp.arange(rows_sec, dtype=jnp.int32)
    is_pivot = jnp.any(parent_pivots[None, :] == my_blocks[:, None], axis=1)
    row_pivot = jnp.repeat(is_pivot, BLK)
    trailing = jnp.where(row_pivot[:, None], jnp.zeros_like(parent_factor), parent_factor)
    offset = dev_index * cols_dev % rows_sec * BLK
    root_sec = dev_index * cols_dev // rows_sec
    column_rows = lax.dynamic_slice_in_dim(trailing, offset, col_width, 0)
    column_factor = spread_2(column_rows, "sec", root_sec)
    parent_update = assembled - outer_rows(trailing, column_factor)
    return (parent_update, parent_factor)


def solution(mesh):
    placed = (P("sec", "dev", None), P("sec", None, None), P(), P("sec", "dev"), P(), P())
    return jax.shard_map(
        local,
        mesh=mesh,
        in_specs=placed,
        out_specs=(P("sec", "dev"), P("sec", None)),
        check_vma=False,
    )
```

profile of v0, /device:TPU:0, one launch (start us, length us, event | category | flops | bytes accessed | tf_op | source)
XLA Modules:
  0.0 718.1 jit_solution(14454594119042678381)
XLA Ops:
  7.2 0.0 copy-start
  7.2 0.0 all-gather.2.cloned.1.call-start
  7.2 1.8 copy-done
  9.1 10.2 %fusion.19 = bf16[768,2048]{1,0:T(8,128)(2,1)} fusion(bf16[1,2048,2048]{2,1,0:T(8,128)(2,1)} %param.7, bf16[1,768,2048]{2,1,0:T(8,128)(2,1)S(1)} %copy-done), kind=kOutput, calls=%fused_computation.15 | convolution fusion | flops 6444023808 | bytes 14680064 | tf_op jit(solution)/shard_map/dot_general | solution.py:35
  19.2 0.0 all-gather.2.cloned.1.call-update
  19.3 0.0 reduce-scatter.2.cloned.1.call-start
  19.3 0.7 dynamic-slice_bitcast_fusion
  20.0 222.0 %all-gather.2.cloned.1.call-done = bf16[6144,2048]{1,0:T(8,128)(2,1)} async-done(((bf16[768,2048]{1,0:T(8,128)(2,1)}), bf16[6144,2048]{1,0:T(8,128)(2,1)}) %all-gather.2.cloned.1.call-update) | async-done | bytes 25165840 | tf_op jit(solution)/shard_map/all_gather | solution.py:39
  242.0 39.9 %fusion.16 = bf16[8,128,2048]{2,0,1:T(8,128)(2,1)S(1)} fusion(bf16[48,128,2048]{2,1,0:T(8,128)(2,1)} %bitcast.33, s32[48]{0:T(128)S(1)} %dynamic-slice_bitcast_fusion, s32[8]{0:T(128)S(1)} %iota_add_fusion.1), kind=kOutput, calls=%fused_computation.14 | convolution fusion | flops 203424128 | bytes 29360352 | tf_op jit(solution)/shard_map/mj,jbp->mbp/dot_general | solution.py:41
  281.9 2.3 copy.18
  284.2 31.7 %negate_convert_fusion = bf16[6144,1024]{1,0:T(8,128)(2,1)} fusion(bf16[6144,2048]{1,0:T(8,128)(2,1)} %all-gather.2.cloned.1.call-done, bf16[1024,2048]{1,0:T(8,128)(2,1)S(1)} %bitcast.35), kind=kOutput, calls=%fused_computation.2 | convolution fusion | flops 25782386688 | bytes 41943040 | tf_op jit(solution)/shard_map/dot_general | solution.py:16
  315.8 25.8 %fusion.4 = bf16[64,128,1024]{2,0,1:T(8,128)(2,1)} fusion(bf16[48,128,1024]{2,1,0:T(8,128)(2,1)} %bitcast.34, s32[48]{0:T(128)S(1)} %dynamic-slice_bitcast_fusion), kind=kOutput, calls=%fused_computation.5 | convolution fusion | flops 813698048 | bytes 29360320 | tf_op jit(solution)/shard_map/jm,jbc->mbc/dot_general | solution.py:48
  341.7 18.6 %copy.20 = bf16[64,128,1024]{2,1,0:T(8,128)(2,1)} copy(bf16[64,128,1024]{2,0,1:T(8,128)(2,1)} %fusion.4) | data formatting | bytes 33554432 | tf_op jit(solution)/shard_map/convert_element_type | solution.py:55
  360.3 0.0 copy-start.4
  360.3 0.0 reduce-scatter.2.cloned.1.call-update
  360.4 0.3 all-reduce.3.cloned.1.call-start
  360.6 0.4 copy-done.4
  361.0 2.9 fusion.25
  363.9 2.5 copy.22
  366.4 146.0 %reduce-scatter.2.cloned.1.call-done = bf16[2048,1024]{1,0:T(8,128)(2,1)} async-done(((bf16[8192,1024]{1,0:T(8,128)(2,1)}), bf16[2048,1024]{1,0:T(8,128)(2,1)}) %reduce-scatter.2.cloned.1.call-update) | async-done | bytes 4194320 | tf_op jit(solution)/shard_map/reduce_scatter | solution.py:54
  512.4 10.6 %fusion.13 = bf16[2048,1024]{1,0:T(8,128)(2,1)} fusion(bf16[1024,1024]{1,0:T(8,128)(2,1)} %bitcast.37, bf16[2048,1024]{1,0:T(8,128)(2,1)} %reduce-scatter.2.cloned.1.call-done, bf16[2048,1024]{1,0:T(8,128)(2,1)} %param.9), kind=kOutput, calls=%fused_computation.13 | convolution fusion | flops 4305453056 | bytes 14680064 | tf_op jit(solution)/shard_map/dot_general | solution.py:67
  523.0 0.0 all-reduce.3.cloned.1.call-update
  523.1 0.0 all-reduce.5.cloned.1.call-start
  523.2 0.1 compare_reduce_fusion
  523.3 0.1 broadcast_bitcast_fusion
  523.3 96.4 %all-reduce.3.cloned.1.call-done = bf16[2048,1024]{1,0:T(8,128)(2,1)} async-done(((bf16[2048,1024]{1,0:T(8,128)(2,1)}), bf16[2048,1024]{1,0:T(8,128)(2,1)}) %all-reduce.3.cloned.1.call-update) | async-done | bytes 4194320 | tf_op jit(solution)/shard_map/psum | solution.py:70
  619.7 2.5 broadcast_select_fusion
  622.2 0.0 copy-start.3
  622.2 2.0 copy-done.3
  624.2 1.8 dynamic-slice_select_fusion
  626.0 0.0 all-reduce.5.cloned.1.call-update
  626.1 69.7 %all-reduce.5.cloned.1.call-done = bf16[1024,1024]{1,0:T(8,128)(2,1)} async-done(((bf16[1024,1024]{1,0:T(8,128)(2,1)}), bf16[1024,1024]{1,0:T(8,128)(2,1)}) %all-reduce.5.cloned.1.call-update) | async-done | bytes 2097168 | tf_op jit(solution)/shard_map/psum | solution.py:12
  695.7 0.0 copy-start.2
  695.8 0.0 copy-start.1
  695.8 13.6 %fusion.9 = f32[2048,1024]{1,0:T(8,128)} fusion(bf16[2048,1024]{1,0:T(8,128)(2,1)} %reduce-scatter.2.cloned.1.call-done, bf16[2048,1024]{1,0:T(8,128)(2,1)} %param.9, bf16[2048,1024]{1,0:T(8,128)(2,1)} %copy-done.3, bf16[1024,1024]{1,0:T(8,128)(2,1)} %all-reduce.5.cloned.1.call-done), kind=kOutput, calls=%fused_computation.9 | convolution fusion | flops 4303355904 | bytes 23068672 | tf_op jit(solution)/shard_map/dot_general | solution.py:16
  709.3 0.0 copy-done.2
  709.3 2.0 copy.37
  711.3 0.0 copy-done.1
  (2 shorter events, 0.0 us)
Async XLA Ops:
  7.2 1.9 copy-start
  7.2 234.8 %all-gather.2.cloned.1.call-start = ((), (), s32[]{:S(2)}) async-start(), calls=%async_computation.1 | async-start | bytes 28311552 | tf_op jit(solution)/shard_map/all_gather | solution.py:39
  19.3 493.2 %reduce-scatter.2.cloned.1.call-start = ((), (), s32[]{:S(2)}) async-start(), calls=%async_computation.2 | async-start | bytes 20971520 | tf_op jit(solution)/shard_map/reduce_scatter | solution.py:54
  360.3 0.7 copy-start.4
  360.4 259.3 %all-reduce.3.cloned.1.call-start = ((), (), s32[]{:S(2)}) async-start(), calls=%async_computation.3 | async-start | bytes 8388608 | tf_op jit(solution)/shard_map/psum | solution.py:70
  523.1 172.7 %all-reduce.5.cloned.1.call-start = ((), (), s32[]{:S(2)}) async-start(), calls=%async_computation.4 | async-start | bytes 4194304 | tf_op jit(solution)/shard_map/psum | solution.py:12
  622.2 2.0 copy-start.3
  695.7 13.6 %copy-start.2 = (bf16[2048,1024]{1,0:T(8,128)(2,1)S(1)}, bf16[2048,1024]{1,0:T(8,128)(2,1)}, u32[]{:S(2)}) copy-start(bf16[2048,1024]{1,0:T(8,128)(2,1)} %all-reduce.3.cloned.1.call-done) | copy-start | bytes 12582916
  695.8 15.6 %copy-start.1 = (bf16[1,768,2048]{2,1,0:T(8,128)(2,1)S(1)}, bf16[1,768,2048]{2,1,0:T(8,128)(2,1)}, u32[]{:S(2)}) copy-start(bf16[1,768,2048]{2,1,0:T(8,128)(2,1)} %param.6) | copy-start | bytes 9437188
Sparse Core Ops, SparseCore 0:
  19.4 222.5 all-gather.1
  360.5 151.9 reduce-scatter.1
  523.2 96.4 all-reduce.2
  626.2 69.5 all-reduce.4
where the time goes:
time: 721 us; the launch traced here: 718 us
  waiting for transfers between devices  534 us (74%)
  matrix products  135 us (19%)
  local copies, waits for them, and re-layouts  30.4 us (4%)
  between operations  14.1 us (2%)
    all_gather x1, waiting for transfers between devices, local(): whole_rows = lax.all_gather(lower_rows, 'dev', axis=0, tiled=True)  222 us
    reduce_scatter x1, waiting for transfers between devices, local(): lax.psum_scatter(spread.astype(jnp.bfloat16), 'sec', scatter_dimension=0,...  146 us
    psum x1, waiting for transfers between devices, local(): parent_factor = lax.psum(partial_sum.astype(jnp.bfloat16), 'dev')  96.4 us
    psum x1, waiting for transfers between devices, spread_2(): return lax.psum(kept, axis)  69.7 us
    dot_general x2, matrix products, outer_rows(): lax.dot_general(left_rows, right_rows, (((1,), (1,)), ((), ())), preferre...  45.2 us
    dot_general x1, matrix products, local(): jnp.einsum('mj,jbp->mbp', pick_cols, whole_rows.reshape(child_blocks, BLK...  39.9 us
    dot_general x1, matrix products, local(): jnp.einsum('jm,jbc->mbc', place_map, by_columns.reshape(child_blocks, BLK...  25.8 us
    convert_element_type x1, local copies, waits for them, and re-layouts, local(): spread.astype(jnp.bfloat16)  18.6 us
  transfers between devices with their start and end apart: 4, of which 4 were waited for; matrix products, arithmetic and copies ran while one was open for 1% of the time, Pallas kernels for 0%

commit v1 on v0

--- a/solution.py
+++ b/solution.py
@@ -9,7 +9,7 @@
 
 def spread_2(value, axis, source):
     kept = jnp.where(lax.axis_index(axis) == source, value, 0).astype(value.dtype)
-    return lax.psum(kept, axis)
+    return jnp.sum(lax.all_gather(kept, axis), axis=0)
 
 
 def outer_rows(left_rows, right_rows):

time: 721 us -> 747 us (1.036)
  waiting for transfers between devices: 534 us -> 552 us
  other arithmetic: 4.4 us -> 11.9 us
    all_gather x0 -> x1, waiting for transfers between devices: none -> 87.7 us  [spread_2(): return jnp.sum(lax.all_gather(kept, axis), axis=0)]
    psum x1 -> x0, waiting for transfers between devices: 69.7 us -> none  [spread_2(): return lax.psum(kept, axis)]
where the time goes in v1:
time: 747 us; the launch traced here: 744 us
  waiting for transfers between devices  552 us (74%)
  matrix products  135 us (18%)
  local copies, waits for them, and re-layouts  30.4 us (4%)
  between operations  14.1 us (2%)
  other arithmetic  11.9 us (2%)
    all_gather x1, waiting for transfers between devices, local(): whole_rows = lax.all_gather(lower_rows, 'dev', axis=0, tiled=True)  222 us
    reduce_scatter x1, waiting for transfers between devices, local(): lax.psum_scatter(spread.astype(jnp.bfloat16), 'sec', scatter_dimension=0,...  146 us
    psum x1, waiting for transfers between devices, local(): parent_factor = lax.psum(partial_sum.astype(jnp.bfloat16), 'dev')  96.1 us
    all_gather x1, waiting for transfers between devices, spread_2(): return jnp.sum(lax.all_gather(kept, axis), axis=0)  87.7 us
    dot_general x2, matrix products, outer_rows(): lax.dot_general(left_rows, right_rows, (((1,), (1,)), ((), ())), preferre...  45.2 us
    dot_general x1, matrix products, local(): jnp.einsum('mj,jbp->mbp', pick_cols, whole_rows.reshape(child_blocks, BLK...  39.9 us
    dot_general x1, matrix products, local(): jnp.einsum('jm,jbc->mbc', place_map, by_columns.reshape(child_blocks, BLK...  25.8 us
    convert_element_type x1, local copies, waits for them, and re-layouts, local(): spread.astype(jnp.bfloat16)  18.6 us
  transfers between devices with their start and end apart: 4, of which 4 were waited for; matrix products, arithmetic and copies ran while one was open for 1% of the time, Pallas kernels for 0%

profile of v1, /device:TPU:0, one launch (start us, length us, event | category | flops | bytes accessed | tf_op | source)
XLA Modules:
  0.0 743.6 jit_solution(17383165399425119231)
XLA Ops:
  7.2 0.0 copy-start
  7.2 0.0 all-gather.4.cloned.1.call-start
  7.2 1.8 copy-done
  9.1 10.2 %fusion.19 = bf16[768,2048]{1,0:T(8,128)(2,1)} fusion(bf16[1,2048,2048]{2,1,0:T(8,128)(2,1)} %param.7, bf16[1,768,2048]{2,1,0:T(8,128)(2,1)S(1)} %copy-done), kind=kOutput, calls=%fused_computation.15 | convolution fusion | flops 6444023808 | bytes 14680064 | tf_op jit(solution)/shard_map/dot_general | solution.py:35
  19.2 0.0 all-gather.4.cloned.1.call-update
  19.3 0.0 reduce-scatter.2.cloned.1.call-start
  19.3 0.7 dynamic-slice_bitcast_fusion
  20.0 222.0 %all-gather.4.cloned.1.call-done = bf16[6144,2048]{1,0:T(8,128)(2,1)} async-done(((bf16[768,2048]{1,0:T(8,128)(2,1)}), bf16[6144,2048]{1,0:T(8,128)(2,1)}) %all-gather.4.cloned.1.call-update) | async-done | bytes 25165840 | tf_op jit(solution)/shard_map/all_gather | solution.py:39
  242.0 39.9 %fusion.16 = bf16[8,128,2048]{2,0,1:T(8,128)(2,1)S(1)} fusion(bf16[48,128,2048]{2,1,0:T(8,128)(2,1)} %bitcast.34, s32[48]{0:T(128)S(1)} %dynamic-slice_bitcast_fusion, s32[8]{0:T(128)S(1)} %iota_add_fusion.1), kind=kOutput, calls=%fused_computation.14 | convolution fusion | flops 203424128 | bytes 29360352 | tf_op jit(solution)/shard_map/mj,jbp->mbp/dot_general | solution.py:41
  281.9 2.3 copy.18
  284.2 31.7 %negate_convert_fusion = bf16[6144,1024]{1,0:T(8,128)(2,1)} fusion(bf16[6144,2048]{1,0:T(8,128)(2,1)} %all-gather.4.cloned.1.call-done, bf16[1024,2048]{1,0:T(8,128)(2,1)S(1)} %bitcast.37), kind=kOutput, calls=%fused_computation.2 | convolution fusion | flops 25782386688 | bytes 41943040 | tf_op jit(solution)/shard_map/dot_general | solution.py:16
  315.9 25.8 %fusion.4 = bf16[64,128,1024]{2,0,1:T(8,128)(2,1)} fusion(bf16[48,128,1024]{2,1,0:T(8,128)(2,1)} %bitcast.35, s32[48]{0:T(128)S(1)} %dynamic-slice_bitcast_fusion), kind=kOutput, calls=%fused_computation.5 | convolution fusion | flops 813698048 | bytes 29360320 | tf_op jit(solution)/shard_map/jm,jbc->mbc/dot_general | solution.py:48
  341.7 18.6 %copy.20 = bf16[64,128,1024]{2,1,0:T(8,128)(2,1)} copy(bf16[64,128,1024]{2,0,1:T(8,128)(2,1)} %fusion.4) | data formatting | bytes 33554432 | tf_op jit(solution)/shard_map/convert_element_type | solution.py:55
  360.3 0.0 copy-start.4
  360.3 0.0 reduce-scatter.2.cloned.1.call-update
  360.4 0.3 all-reduce.2.cloned.1.call-start
  360.6 0.4 copy-done.4
  361.0 2.9 fusion.25
  363.9 2.5 copy.22
  366.4 146.0 %reduce-scatter.2.cloned.1.call-done = bf16[2048,1024]{1,0:T(8,128)(2,1)} async-done(((bf16[8192,1024]{1,0:T(8,128)(2,1)}), bf16[2048,1024]{1,0:T(8,128)(2,1)}) %reduce-scatter.2.cloned.1.call-update) | async-done | bytes 4194320 | tf_op jit(solution)/shard_map/reduce_scatter | solution.py:54
  512.4 10.6 %fusion.13 = bf16[2048,1024]{1,0:T(8,128)(2,1)} fusion(bf16[1024,1024]{1,0:T(8,128)(2,1)} %bitcast.39, bf16[2048,1024]{1,0:T(8,128)(2,1)} %reduce-scatter.2.cloned.1.call-done, bf16[2048,1024]{1,0:T(8,128)(2,1)} %param.9), kind=kOutput, calls=%fused_computation.13 | convolution fusion | flops 4305453056 | bytes 14680064 | tf_op jit(solution)/shard_map/dot_general | solution.py:67
  523.0 0.0 all-reduce.2.cloned.1.call-update
  523.1 0.3 all-gather.6.cloned.1.call-start
  523.4 0.1 compare_reduce_fusion
  523.5 0.1 broadcast_bitcast_fusion
  523.6 96.1 %all-reduce.2.cloned.1.call-done = bf16[2048,1024]{1,0:T(8,128)(2,1)} async-done(((bf16[2048,1024]{1,0:T(8,128)(2,1)}), bf16[2048,1024]{1,0:T(8,128)(2,1)}) %all-reduce.2.cloned.1.call-update) | async-done | bytes 4194320 | tf_op jit(solution)/shard_map/psum | solution.py:70
  619.7 2.5 broadcast_select_fusion
  622.2 0.0 copy-start.3
  622.2 2.0 copy-done.3
  624.2 1.8 dynamic-slice_select_fusion
  626.0 0.0 all-gather.6.cloned.1.call-update
  626.1 87.7 %all-gather.6.cloned.1.call-done = bf16[4096,1024]{1,0:T(8,128)(2,1)} async-done(((bf16[1024,1024]{1,0:T(8,128)(2,1)}), bf16[4096,1024]{1,0:T(8,128)(2,1)}) %all-gather.6.cloned.1.call-update) | async-done | bytes 8388624 | tf_op jit(solution)/shard_map/all_gather | solution.py:12
  713.7 7.5 %reduce_sum.12 = bf16[1024,1024]{1,0:T(8,128)(2,1)} reduce(bf16[4,1024,1024]{2,1,0:T(8,128)(2,1)} %bitcast.36, bf16[]{:T(256)} %constant.46.clone.1), dimensions={0}, to_apply=%region_3.4 | reduce | flops 3145728 | bytes 10485762 | tf_op jit(solution)/shard_map/reduce_sum | solution.py:12
  721.2 0.0 copy-start.2
  721.2 0.0 copy-start.1
  721.2 13.6 %fusion.9 = f32[2048,1024]{1,0:T(8,128)} fusion(bf16[2048,1024]{1,0:T(8,128)(2,1)} %reduce-scatter.2.cloned.1.call-done, bf16[2048,1024]{1,0:T(8,128)(2,1)} %param.9, bf16[2048,1024]{1,0:T(8,128)(2,1)} %copy-done.3, bf16[1024,1024]{1,0:T(8,128)(2,1)} %reduce_sum.12), kind=kOutput, calls=%fused_computation.9 | convolution fusion | flops 4303355904 | bytes 23068672 | tf_op jit(solution)/shard_map/dot_general | solution.py:16
  734.8 0.0 copy-done.2
  734.8 2.0 copy.36
  736.8 0.0 copy-done.1
  (2 shorter events, 0.0 us)
Async XLA Ops:
  7.2 1.9 copy-start
  7.2 234.8 %all-gather.4.cloned.1.call-start = ((), (), s32[]{:S(2)}) async-start(), calls=%async_computation.1 | async-start | bytes 28311552 | tf_op jit(solution)/shard_map/all_gather | solution.py:39
  19.3 493.2 %reduce-scatter.2.cloned.1.call-start = ((), (), s32[]{:S(2)}) async-start(), calls=%async_computation.2 | async-start | bytes 20971520 | tf_op jit(solution)/shard_map/reduce_scatter | solution.py:54
  360.3 0.7 copy-start.4
  360.4 259.3 %all-reduce.2.cloned.1.call-start = ((), (), s32[]{:S(2)}) async-start(), calls=%async_computation.3 | async-start | bytes 8388608 | tf_op jit(solution)/shard_map/psum | solution.py:70
  523.1 190.7 %all-gather.6.cloned.1.call-start = ((), (), s32[]{:S(2)}) async-start(), calls=%async_computation.4 | async-start | bytes 10485760 | tf_op jit(solution)/shard_map/all_gather | solution.py:12
  622.2 2.0 copy-start.3
  721.2 13.6 %copy-start.2 = (bf16[2048,1024]{1,0:T(8,128)(2,1)S(1)}, bf16[2048,1024]{1,0:T(8,128)(2,1)}, u32[]{:S(2)}) copy-start(bf16[2048,1024]{1,0:T(8,128)(2,1)} %all-reduce.2.cloned.1.call-done) | copy-start | bytes 12582916
  721.2 15.6 %copy-start.1 = (bf16[1,768,2048]{2,1,0:T(8,128)(2,1)S(1)}, bf16[1,768,2048]{2,1,0:T(8,128)(2,1)}, u32[]{:S(2)}) copy-start(bf16[1,768,2048]{2,1,0:T(8,128)(2,1)} %param.6) | copy-start | bytes 9437188
Sparse Core Ops, SparseCore 0:
  19.4 222.5 all-gather.3
  360.5 151.8 reduce-scatter.1
  523.2 96.4 all-reduce.1
  626.2 87.5 all-gather.5
